TPU v7x, 32 devices: a whole 2x2x4 slice. The times are simulated.
32 devices in a mesh: ctx: 8 (over z, x), ch: 4 (over y, core).
Axes of the slice: x: 2, y: 2, z: 4, core: 2. Of those that a mesh axis runs over, the one named last changes fastest.
Arguments:
- tokens: bfloat16 [2048, 4096], P('ctx', 'ch'), may hold values from -6 to 6
- in_weight: bfloat16 [4096, 3, 4096], P('ch', None, 'ctx'), may hold values from -0.09375 to 0.09375
- short_filter: float32 [4096, 3, 3], P('ch'), may hold values from -3 to 3
- decay_rates: float32 [4096, 16], P('ch'), may hold values from 0.00024414062 to 0.05
- residues: float32 [4096, 16], P('ch'), may hold values from -1.5 to 1.5
- skip_gain: float32 [4096], P('ch'), may hold values from -4 to 4
- out_weight: bfloat16 [4096, 4096], P(None, 'ch'), may hold values from -0.09375 to 0.09375
Outputs:
- mixed: bfloat16 [2048, 4096], P('ctx', 'ch')
All inputs are finite; a program needn't handle non-finite values.
Results may differ from a plain program's by a relative error of at most 0.02.
Values may be sent and summed in bfloat16 or wider, within the bound.
A program may use at most 320 MiB of HBM per device.

v0:
```python
import jax
import jax.numpy as jnp
from jax import lax
from jax.sharding import PartitionSpec as P

HIGHEST = lax.Precision.HIGHEST


def shifted(x, axis, by):
    size = lax.axis_size(axis)
    pairs = [(i, i + by) for i in range(size) if 0 <= i + by < size]
    return lax.ppermute(x, axis, pairs)


def local_conv(product, decay_rates, residues, span):
    chans, length = product.shape
    blocks = length // span
    mode_gain = residues * jnp.sqrt(-jnp.expm1(-2.0 * decay_rates))
    offsets = jnp.arange(span).astype(jnp.float32)
    falling = mode_gain[:, :, None] * jnp.exp(-decay_rates[:, :, None] * offsets)
    rising = jnp.exp(decay_rates[:, :, None] * offsets)
    toeplitz = jnp.einsum("cnt,cns->cts", falling, rising, precision=HIGHEST)
    lower = offsets[:, None] >= offsets[None, :]
    toeplitz = jnp.where(lower[None], toeplitz, 0.0)
    carry_in = mode_gain[:, :, None] * jnp.exp(-decay_rates[:, :, None] * (offsets + 1.0))
    carry_out = jnp.exp(-decay_rates[:, :, None] * (span - 1.0 - offsets))
    through = jnp.exp(-decay_rates * span)
    pieces = product.reshape(chans, blocks, span).transpose(1, 0, 2).astype(jnp.float32)
    within = jnp.einsum("cts,bcs->bct", toeplitz, pieces, precision=HIGHEST)
    injected = jnp.einsum("cns,bcs->bcn", carry_out, pieces, precision=HIGHEST)

    def advance(state, added):
        return (through * state + added, state)

    state, before = lax.scan(advance, jnp.zeros(decay_rates.shape, jnp.float32), injected)
    results = within + jnp.einsum("cnt,bcn->bct", carry_in, before, precision=HIGHEST)
    return (results.transpose(1, 0, 2).reshape(chans, length), state)


def local(tokens, in_weight, short_filter, decay_rates, residues, skip_gain, out_weight):
    rows_here = tokens.shape[0]
    terms = jnp.einsum(
        "rd,dsc->csr",
        tokens,
        lax.all_gather(in_weight, "ctx", axis=2, tiled=True),
        preferred_element_type=jnp.float32,
    )
    projected = lax.psum_scatter(terms.astype(jnp.bfloat16), "ch", scatter_dimension=0, tiled=True)
    group = projected.shape[0]
    reach = short_filter.shape[2] - 1
    rim = shifted(projected[:, :, rows_here - reach :], "ctx", 1)
    extended = jnp.concatenate([rim, projected], axis=2)
    featured = jnp.zeros(projected.shape, jnp.float32)
    for shift_by in range(reach + 1):
        begin = reach - shift_by
        featured = featured + short_filter[:, :, shift_by, None] * extended[
            :, :, begin : begin + rows_here
        ].astype(jnp.float32)
    query = featured[:, 0]
    product = (featured[:, 1] * featured[:, 2]).astype(jnp.bfloat16)
    count = lax.axis_size("ctx")
    chans = group // count
    sent = product.reshape(count, chans, rows_here)
    whole = lax.all_to_all(sent, "ctx", split_axis=0, concat_axis=2, tiled=True)
    length = whole.shape[2]
    start = lax.axis_index("ctx") * chans
    mine_rates = lax.dynamic_slice_in_dim(decay_rates, start, chans, 0)
    mine_residues = lax.dynamic_slice_in_dim(residues, start, chans, 0)
    full_out, final_state = local_conv(
        whole.reshape(chans, length), mine_rates, mine_residues, min(512, length)
    )
    back = lax.all_to_all(
        full_out.reshape(1, chans, length).astype(jnp.bfloat16),
        "ctx",
        split_axis=2,
        concat_axis=0,
        tiled=True,
    ).astype(jnp.float32)
    convolved = back.reshape(group, rows_here)
    gated = (query * (convolved + skip_gain[:, None] * product.astype(jnp.float32))).astype(
        jnp.bfloat16
    )
    mixed = lax.dot_general(
        lax.all_gather(gated, "ch", axis=0, tiled=True),
        out_weight,
        (((0,), (0,)), ((), ())),
        preferred_element_type=jnp.float32,
    )
    return mixed.astype(jnp.bfloat16)


def solution(mesh):
    in_specs = (
        P("ctx", "ch"),
        P("ch", None, "ctx"),
        P("ch", None, None),
        P("ch", None),
        P("ch", None),
        P("ch"),
        P(None, "ch"),
    )
    out_specs = P("ctx", "ch")
    return jax.shard_map(local, mesh=mesh, in_specs=in_specs, out_specs=out_specs, check_vma=False)
```

profile of v0, /device:TPU:0, one launch (start us, length us, event | category | flops | bytes accessed | tf_op | source)
XLA Modules:
  0.0 852.0 jit_solution(11152898393615489229)
XLA Ops:
  6.5 0.0 copy-start
  6.5 0.0 all-gather.3.cloned.1.call-start
  6.5 4.7 copy.22
  11.3 0.0 all-gather.3.cloned.1.call-update
  11.3 0.0 reduce-scatter.2.cloned.1.call-start
  11.3 483.2 %all-gather.3.cloned.1.call-done = bf16[1024,3,4096]{0,2,1:T(8,128)(2,1)} async-done(((bf16[1024,3,512]{0,2,1:T(8,128)(2,1)}), bf16[1024,3,4096]{0,2,1:T(8,128)(2,1)}) %all-gather.3.cloned.1.call-update) | async-done | bytes 25165840 | tf_op jit(solution)/shard_map/all_gather | solution.py:45
  494.6 0.0 copy-done
  494.6 13.3 %fusion.4 = bf16[4096,3,256]{2,0,1:T(8,128)(2,1)} fusion(bf16[1024,3,4096]{0,2,1:T(8,128)(2,1)} %all-gather.3.cloned.1.call-done, bf16[256,1024]{1,0:T(8,128)(2,1)S(1)} %copy-done), kind=kOutput, calls=%fused_computation.7 | convolution fusion | flops 6445596672 | bytes 31981568 | tf_op jit(solution)/shard_map/rd,dsc->csr/dot_general | solution.py:42
  507.9 0.0 copy-start.4
  507.9 0.0 reduce-scatter.2.cloned.1.call-update
  507.9 0.7 multiply_exponential_fusion
  508.6 0.7 sqrt_multiply_fusion
  509.3 0.0 copy-done.4
  509.4 57.0 %reduce-scatter.2.cloned.1.call-done = bf16[1024,3,256]{2,0,1:T(8,128)(2,1)} async-done(((bf16[4096,3,256]{2,0,1:T(8,128)(2,1)}), bf16[1024,3,256]{2,0,1:T(8,128)(2,1)}) %reduce-scatter.2.cloned.1.call-update) | async-done | bytes 1572880 | tf_op jit(solution)/shard_map/reduce_scatter | solution.py:48
  566.4 0.0 copy-start.3
  566.4 1.5 slice.36
  567.9 0.3 copy.23
  568.2 3.3 collective-permute-start
  571.6 0.1 copy.28
  571.7 0.1 copy.27
  571.8 0.1 copy.26
  571.9 1.1 collective-permute-done
  573.0 0.4 copy.24
  573.4 0.0 copy-done.3
  573.4 2.6 multiply_add_fusion
  576.0 0.0 copy-start.2
  576.1 1.6 copy-done.2
  577.7 0.9 fusion.37
  578.6 6.4 all-to-all-start
  584.9 0.0 all-gather.5.cloned.1.call-start
  585.0 118.0 %fusion.12 = f32[128,512,512]{2,1,0:T(8,128)} fusion(f32[128,16]{1,0:T(8,128)S(1)} %copy.28, f32[512]{0:T(512)S(1)} %iota_convert_fusion, f32[128,16]{1,0:T(8,128)S(1)} %copy.27, f32[128,16]{1,0:T(8,128)S(1)} %copy.26), kind=kOutput, calls=%fused_computation.15 | convolution fusion | flops 6445596672 | bytes 134244352 | tf_op jit(solution)/shard_map/cnt,cns->cts/dot_general | solution.py:22
  703.0 0.2 broadcast_compare_fusion
  703.3 0.0 all-to-all-done
  703.3 0.3 copy.25
  703.6 0.3 reshape_reshape.4
  703.9 2.8 fusion.34
  706.7 0.1 copy.29
  706.8 0.2 while.13
  707.0 0.1 copy.30
  707.1 71.1 %fusion = f32[128,4,512]{2,1,0:T(4,128)S(1)} fusion(f32[128,512,512]{2,1,0:T(8,128)} %fusion.12, pred[512,512]{1,0:T(8,128)(4,1)S(1)} %broadcast_compare_fusion, bf16[128,4,512]{2,1,0:T(4,128)(2,1)S(1)} %reshape_reshape.4), kind=kOutput, calls=%fused_computation.2 | convolution fusion | flops 1644167168 | bytes 136052736 | tf_op jit(solution)/shard_map/cts,bcs->bct/dot_general | solution.py:29
  778.2 2.9 fusion.31
  781.2 0.4 convert_element_type.101
  781.5 0.8 copy.31
  782.3 0.5 broadcast.38
  782.8 11.7 %reduce = bf16[2048,128]{1,0:T(8,128)(2,1)S(1)} reduce(bf16[2048,1,128]{2,1,0:T(2,128)(2,1)S(1)} %bitcast.55, bf16[]{:T(256)} %broadcast.38), dimensions={1}, to_apply=%bitcast.43.reduce_sub_computation | reduce | bytes 1048578
  794.6 0.1 reshape.83
  794.7 0.0 copy-start.5
  794.7 18.5 %all_to_all.24 = bf16[8,2,16384]{2,1,0:T(2,128)(2,1)S(1)} all-to-all(bf16[8,2,16384]{2,1,0:T(2,128)(2,1)S(1)} %reshape.83), channel_id=1, replica_groups=mesh['ctx'=8,'ch'=4] {'ctx'}, dimensions={0} | all-to-all | bytes 1048576 | tf_op jit(solution)/shard_map/all_to_all | solution.py:72
  813.2 0.5 reshape.84
  813.7 0.1 copy.32
  813.8 0.1 convert_bitcast_fusion
  813.9 0.3 copy.33
  814.2 0.0 copy-done.5
  814.2 2.9 fusion.39
  817.1 0.0 all-gather.5.cloned.1.call-update
  817.2 20.9 %all-gather.5.cloned.1.call-done = bf16[4096,256]{1,0:T(8,128)(2,1)} async-done(((bf16[1024,256]{1,0:T(8,128)(2,1)}), bf16[4096,256]{1,0:T(8,128)(2,1)}) %all-gather.5.cloned.1.call-update) | async-done | bytes 2097168 | tf_op jit(solution)/shard_map/all_gather | solution.py:84
  838.0 0.0 copy-start.1
  838.0 7.2 convolution_convert_fusion.1
  845.3 0.0 copy-done.1
  (16 shorter events, 0.1 us)
Async XLA Ops:
  6.5 488.1 %copy-start = (bf16[256,1024]{1,0:T(8,128)(2,1)S(1)}, bf16[256,1024]{1,0:T(8,128)(2,1)}, u32[]{:S(2)}) copy-start(bf16[256,1024]{1,0:T(8,128)(2,1)} %param.9) | copy-start | bytes 1572868
  6.5 488.0 %all-gather.3.cloned.1.call-start = ((), (), s32[]{:S(2)}) async-start(), calls=%async_computation.3 | async-start | bytes 28311552 | tf_op jit(solution)/shard_map/all_gather | solution.py:45
  11.3 555.1 %reduce-scatter.2.cloned.1.call-start = ((), (), s32[]{:S(2)}) async-start(), calls=%async_computation.4 | async-start | bytes 7864320 | tf_op jit(solution)/shard_map/reduce_scatter | solution.py:48
  507.9 1.5 copy-start.4
  566.4 7.0 copy-start.3
  568.2 4.7 collective-permute-start
  576.0 1.6 copy-start.2
  578.6 124.7 %all-to-all-start = ((bf16[8,128,256]{2,1,0:T(8,128)(2,1)}), bf16[8,128,256]{2,1,0:T(8,128)(2,1)S(1)}, u32[]{:S(2)}, u32[]{:S(2)}) async-start(bf16[8,128,256]{2,1,0:T(8,128)(2,1)} %bitcast.3), calls=%async_computation.1 | async-start | bytes 1048576 | tf_op jit(solution)/shard_map/all_to_all | solution.py:64
  584.9 253.1 %all-gather.5.cloned.1.call-start = ((), (), s32[]{:S(2)}) async-start(), calls=%async_computation.5 | async-start | bytes 2621440 | tf_op jit(solution)/shard_map/all_gather | solution.py:84
  794.7 19.5 %copy-start.5 = (f32[1024]{0:T(1024)S(1)}, f32[1024]{0:T(1024)}, u32[]{:S(2)}) copy-start(f32[1024]{0:T(1024)} %param.14) | copy-start | bytes 12292
  838.0 7.2 copy-start.1
Sparse Core Ops, SparseCore 0:
  11.4 483.1 all-gather.2
  508.0 58.3 reduce-scatter.1
  817.3 20.7 all-gather.4
where the time goes:
time: 857 us; the launch traced here: 852 us
  waiting for transfers between devices  562 us (66%)
  matrix products  215 us (25%)
  other arithmetic  20 us (2%)
  blocking collectives  18.5 us (2%)
  between operations  13.6 us (2%)
  local copies, waits for them, and re-layouts  12.5 us (1%)
  starting transfers between devices  9.78 us (1%)
    all_gather x1, waiting for transfers between devices, local(): lax.all_gather(in_weight, 'ctx', axis=2, tiled=True)  483 us
    dot_general x1, matrix products, local_conv(): toeplitz = jnp.einsum('cnt,cns->cts', falling, rising, precision=HIGHEST)  118 us
    dot_general x1, matrix products, local_conv(): within = jnp.einsum('cts,bcs->bct', toeplitz, pieces, precision=HIGHEST)  71.1 us
    reduce_scatter x1, waiting for transfers between devices, local(): lax.psum_scatter(terms.astype(jnp.bfloat16), 'ch', scatter_dimension=0, t...  57 us
    all_gather x1, waiting for transfers between devices, local(): lax.all_gather(gated, 'ch', axis=0, tiled=True)  20.9 us
    all_to_all x1, blocking collectives, local(): lax.all_to_all(full_out.reshape(1, chans, length).astype(jnp.bfloat16), '...  18.5 us
  transfers between devices with their start and end apart: 5, of which 4 were waited for; matrix products, arithmetic and copies ran while one was open for 14% of the time, Pallas kernels for 0%

commit v1 on v0

--- a/solution.py
+++ b/solution.py
@@ -69,12 +69,20 @@
     full_out, final_state = local_conv(
         whole.reshape(chans, length), mine_rates, mine_residues, min(512, length)
     )
-    back = lax.all_to_all(
-        full_out.reshape(1, chans, length).astype(jnp.bfloat16),
-        "ctx",
-        split_axis=2,
-        concat_axis=0,
-        tiled=True,
+    back = jnp.concatenate(
+        lax.all_to_all(
+            jnp.stack(
+                jnp.split(
+                    full_out.reshape(1, chans, length).astype(jnp.bfloat16),
+                    lax.axis_size("ctx"),
+                    axis=2,
+                )
+            ),
+            "ctx",
+            0,
+            0,
+        ),
+        axis=0,
     ).astype(jnp.float32)
     convolved = back.reshape(group, rows_here)
     gated = (query * (convolved + skip_gain[:, None] * product.astype(jnp.float32))).astype(

time: 857 us -> 837 us (0.977)
  other arithmetic: 20 us -> 8.18 us
    unnamed x2 -> x1, other arithmetic: 11.7 us -> 0.01 us
where the time goes in v1:
time: 837 us
  waiting for transfers between devices  562 us (67%)
  matrix products  215 us (26%)
  blocking collectives  18.3 us (2%)
  between operations  13.3 us (2%)
  local copies, waits for them, and re-layouts  10.3 us (1%)
  starting transfers between devices  9.78 us (1%)
    all_gather x1, waiting for transfers between devices, local(): lax.all_gather(in_weight, 'ctx', axis=2, tiled=True)  483 us
    dot_general x1, matrix products, local_conv(): toeplitz = jnp.einsum('cnt,cns->cts', falling, rising, precision=HIGHEST)  118 us
    dot_general x1, matrix products, local_conv(): within = jnp.einsum('cts,bcs->bct', toeplitz, pieces, precision=HIGHEST)  71.1 us
    reduce_scatter x1, waiting for transfers between devices, local(): lax.psum_scatter(terms.astype(jnp.bfloat16), 'ch', scatter_dimension=0, t...  57 us
    all_gather x1, waiting for transfers between devices, local(): lax.all_gather(gated, 'ch', axis=0, tiled=True)  20.9 us
    all_to_all x1, blocking collectives, local(): lax.all_to_all(jnp.stack(jnp.split(full_out.reshape(1, chans, length).ast...  18.3 us
  transfers between devices with their start and end apart: 5, of which 4 were waited for; matrix products, arithmetic and copies ran while one was open for 14% of the time, Pallas kernels for 0%

profile of v1, /device:TPU:0, one launch (start us, length us, event | category | flops | bytes accessed | tf_op | source)
XLA Modules:
  0.0 837.0 jit_solution(13044500700583044399)
XLA Ops:
  6.5 0.0 copy-start
  6.5 0.0 all-gather.3.cloned.1.call-start
  6.5 4.7 copy.34
  11.2 0.0 all-gather.3.cloned.1.call-update
  11.3 0.0 reduce-scatter.2.cloned.1.call-start
  11.3 483.2 %all-gather.3.cloned.1.call-done = bf16[1024,3,4096]{0,2,1:T(8,128)(2,1)} async-done(((bf16[1024,3,512]{0,2,1:T(8,128)(2,1)}), bf16[1024,3,4096]{0,2,1:T(8,128)(2,1)}) %all-gather.3.cloned.1.call-update) | async-done | bytes 25165840 | tf_op jit(solution)/shard_map/all_gather | solution.py:45
  494.6 0.0 copy-done
  494.6 13.3 %fusion.4 = bf16[4096,3,256]{2,0,1:T(8,128)(2,1)} fusion(bf16[1024,3,4096]{0,2,1:T(8,128)(2,1)} %all-gather.3.cloned.1.call-done, bf16[256,1024]{1,0:T(8,128)(2,1)S(1)} %copy-done), kind=kOutput, calls=%fused_computation.7 | convolution fusion | flops 6445596672 | bytes 31981568 | tf_op jit(solution)/shard_map/rd,dsc->csr/dot_general | solution.py:42
  507.9 0.0 copy-start.3
  507.9 0.0 reduce-scatter.2.cloned.1.call-update
  507.9 0.7 multiply_exponential_fusion
  508.6 0.7 sqrt_multiply_fusion
  509.3 0.0 copy-done.3
  509.4 57.0 %reduce-scatter.2.cloned.1.call-done = bf16[1024,3,256]{2,0,1:T(8,128)(2,1)} async-done(((bf16[4096,3,256]{2,0,1:T(8,128)(2,1)}), bf16[1024,3,256]{2,0,1:T(8,128)(2,1)}) %reduce-scatter.2.cloned.1.call-update) | async-done | bytes 1572880 | tf_op jit(solution)/shard_map/reduce_scatter | solution.py:48
  566.4 0.0 copy-start.2
  566.4 1.5 slice.36
  567.9 0.3 copy.35
  568.2 3.4 collective-permute-start
  571.6 0.1 copy.40
  571.7 0.1 copy.39
  571.8 0.1 copy.38
  571.9 1.1 collective-permute-done
  573.0 0.4 copy.36
  573.4 0.0 copy-done.2
  573.4 2.6 multiply_add_fusion
  576.0 0.0 copy-start.1
  576.0 1.6 copy-done.1
  577.7 0.9 fusion.37
  578.6 6.3 all-to-all-start
  584.9 0.0 all-gather.5.cloned.1.call-start
  584.9 117.6 %fusion.12 = f32[128,512,512]{2,1,0:T(8,128)} fusion(f32[128,16]{1,0:T(8,128)S(1)} %copy.40, f32[512]{0:T(512)S(1)} %iota_convert_fusion, f32[128,16]{1,0:T(8,128)S(1)} %copy.39, f32[128,16]{1,0:T(8,128)S(1)} %copy.38), kind=kOutput, calls=%fused_computation.15 | convolution fusion | flops 6445596672 | bytes 134244352 | tf_op jit(solution)/shard_map/cnt,cns->cts/dot_general | solution.py:22
  702.5 0.2 broadcast_compare_fusion
  702.7 0.0 all-to-all-done
  702.7 0.3 copy.37
  703.0 0.3 reshape_reshape.4
  703.4 2.8 fusion.34
  706.1 0.1 copy.41
  706.2 0.2 while.13
  706.4 0.1 copy.42
  706.6 71.1 %fusion = f32[128,4,512]{2,1,0:T(4,128)S(1)} fusion(f32[128,512,512]{2,1,0:T(8,128)} %fusion.12, pred[512,512]{1,0:T(8,128)(4,1)S(1)} %broadcast_compare_fusion, bf16[128,4,512]{2,1,0:T(4,128)(2,1)S(1)} %reshape_reshape.4), kind=kOutput, calls=%fused_computation.2 | convolution fusion | flops 1644167168 | bytes 136052736 | tf_op jit(solution)/shard_map/cts,bcs->bct/dot_general | solution.py:29
  777.7 0.0 copy-start.4
  777.7 2.9 fusion.31
  780.6 0.4 convert_element_type.95
  781.2 18.3 %all_to_all.20 = bf16[8,1,128,256]{3,2,1,0:T(8,128)(2,1)S(1)} all-to-all(bf16[8,1,128,256]{3,2,1,0:T(8,128)(2,1)S(1)} %fusion.44), channel_id=1, replica_groups=mesh['ctx'=8,'ch'=4] {'ctx'}, dimensions={0} | all-to-all | bytes 1048576 | tf_op jit(solution)/shard_map/all_to_all | solution.py:73
  799.5 0.0 copy-done.4
  799.5 2.9 fusion.39
  802.4 0.0 all-gather.5.cloned.1.call-update
  802.4 20.9 %all-gather.5.cloned.1.call-done = bf16[4096,256]{1,0:T(8,128)(2,1)} async-done(((bf16[1024,256]{1,0:T(8,128)(2,1)}), bf16[4096,256]{1,0:T(8,128)(2,1)}) %all-gather.5.cloned.1.call-update) | async-done | bytes 2097168 | tf_op jit(solution)/shard_map/all_gather | solution.py:92
  823.3 7.2 convolution_convert_fusion.1
  (24 shorter events, 0.2 us)
Async XLA Ops:
  6.5 488.0 %copy-start = (bf16[256,1024]{1,0:T(8,128)(2,1)S(1)}, bf16[256,1024]{1,0:T(8,128)(2,1)}, u32[]{:S(2)}) copy-start(bf16[256,1024]{1,0:T(8,128)(2,1)} %param.9) | copy-start | bytes 1572868
  6.5 488.0 %all-gather.3.cloned.1.call-start = ((), (), s32[]{:S(2)}) async-start(), calls=%async_computation.3 | async-start | bytes 28311552 | tf_op jit(solution)/shard_map/all_gather | solution.py:45
  11.3 555.1 %reduce-scatter.2.cloned.1.call-start = ((), (), s32[]{:S(2)}) async-start(), calls=%async_computation.4 | async-start | bytes 7864320 | tf_op jit(solution)/shard_map/reduce_scatter | solution.py:48
  507.9 1.5 copy-start.3
  566.4 7.0 copy-start.2
  568.2 4.8 collective-permute-start
  576.0 1.6 copy-start.1
  578.6 124.2 %all-to-all-start = ((bf16[8,128,256]{2,1,0:T(8,128)(2,1)}), bf16[8,128,256]{2,1,0:T(8,128)(2,1)S(1)}, u32[]{:S(2)}, u32[]{:S(2)}) async-start(bf16[8,128,256]{2,1,0:T(8,128)(2,1)} %bitcast.3), calls=%async_computation.1 | async-start | bytes 1048576 | tf_op jit(solution)/shard_map/all_to_all | solution.py:64
  584.9 238.4 %all-gather.5.cloned.1.call-start = ((), (), s32[]{:S(2)}) async-start(), calls=%async_computation.5 | async-start | bytes 2621440 | tf_op jit(solution)/shard_map/all_gather | solution.py:92
  777.7 21.8 %copy-start.4 = (f32[1024]{0:T(1024)S(1)}, f32[1024]{0:T(1024)}, u32[]{:S(2)}) copy-start(f32[1024]{0:T(1024)} %param.14) | copy-start | bytes 12292
Sparse Core Ops, SparseCore 0:
  11.4 483.1 all-gather.2
  508.0 58.3 reduce-scatter.1
  802.6 20.7 all-gather.4
